TPU v7x, 128 devices: a whole 4x4x4 slice. The times are simulated.
128 devices in a mesh: erow: 8 (over x, core), ecol: 16 (over z, y).
Axes of the slice: x: 4, y: 4, z: 4, core: 2. Of those that a mesh axis runs over, the one named last changes fastest.
Arguments:
- tokens: bfloat16 [1024, 7168], P(('erow', 'ecol')), may hold values from -6 to 6
- routes: int32 [1024, 4], P(('erow', 'ecol')), may hold values from 0 to 15, all different within a row; in each aligned block of 8 rows (0 to 7, 8 to 15, ...) at most 4 rows name the same one
- gate_probs: bfloat16 [1024, 4], P(('erow', 'ecol')), may hold values from 0.049804688 to 0.5
- cotangent: bfloat16 [1024, 7168], P(('erow', 'ecol')), may hold values from -0.625 to 0.625
- w_gate_up: bfloat16 [16, 7168, 2, 2048], P('ecol', 'erow'), may hold values from -0.0625 to 0.0625
- w_down: bfloat16 [16, 2048, 7168], P('ecol', None, 'erow'), may hold values from -0.125 to 0.125
Outputs:
- layer_out: bfloat16 [1024, 7168], P(('erow', 'ecol'))
- grad_tokens: bfloat16 [1024, 7168], P(('erow', 'ecol'))
- grad_probs: float32 [1024, 4], P(('erow', 'ecol'))
- grad_gate_up: bfloat16 [16, 7168, 2, 2048], P('ecol', 'erow')
- grad_down: bfloat16 [16, 2048, 7168], P('ecol', None, 'erow')
Inputs may be any that keep to these rules, and one draw needn't show every extreme that they name: `routes`: each row names 4 different experts; among the 8 rows of one device no expert is named more than 4 times, and in some device's rows an expert is named exactly 4 times.
All inputs are finite; a program needn't handle non-finite values.
Results may differ from a plain program's by a relative error of at most 0.039.
Values may be sent and summed in bfloat16 or wider, within the bound.
A program may use at most 128 MiB of HBM per device.

v0:
```python
import jax
import jax.numpy as jnp
from jax import lax
from jax.sharding import PartitionSpec as P


def send_rows(place_flat, slot_probs, tokens, cotangent, n_row, experts, capacity):
    token_count = tokens.shape[0]
    weight_slice = tokens.shape[1] // n_row
    token_parts = tokens.reshape(token_count, n_row, weight_slice)
    cot_parts = cotangent.reshape(token_count, n_row, weight_slice)
    x_out = (
        jnp.einsum("ts,trd->rsd", place_flat, token_parts, preferred_element_type=jnp.float32)
        .astype(jnp.bfloat16)
        .reshape(n_row * experts, capacity, weight_slice)
    )
    cot_out = (
        jnp.einsum("ts,trd->rsd", place_flat, cot_parts, preferred_element_type=jnp.float32)
        .astype(jnp.bfloat16)
        .reshape(n_row * experts, capacity, weight_slice)
    )
    prob_out = jnp.broadcast_to(
        slot_probs[None, :, :, None], (n_row, experts, capacity, 1)
    ).reshape(n_row * experts, capacity, 1)
    x_in, cot_in, prob_in = (
        lax.all_to_all(x_out, ("erow", "ecol"), split_axis=0, concat_axis=0, tiled=True),
        lax.all_to_all(cot_out, ("erow", "ecol"), split_axis=0, concat_axis=0, tiled=True),
        lax.all_to_all(prob_out, ("erow", "ecol"), split_axis=0, concat_axis=0, tiled=True),
    )
    return (x_in.reshape(-1, weight_slice), cot_in.reshape(-1, weight_slice), prob_in.reshape(-1))


def return_values(row_values, place_flat, n_row, experts, capacity):
    weight_slice = row_values.shape[1]
    returned = lax.all_to_all(
        row_values.reshape(n_row * experts, capacity, weight_slice),
        ("erow", "ecol"),
        split_axis=0,
        concat_axis=0,
        tiled=True,
    )
    summed = jnp.einsum(
        "ts,rsd->trd",
        place_flat,
        returned.reshape(n_row, experts * capacity, weight_slice),
        preferred_element_type=jnp.float32,
    )
    return summed.reshape(place_flat.shape[0], n_row * weight_slice)


def return_grads(grad_rows, dprob_rows, place_flat, n_row, experts, capacity):
    weight_slice = grad_rows.shape[1]
    returned, returned_prob = (
        lax.all_to_all(
            grad_rows.reshape(n_row * experts, capacity, weight_slice),
            ("erow", "ecol"),
            split_axis=0,
            concat_axis=0,
            tiled=True,
        ),
        lax.all_to_all(
            dprob_rows.reshape(n_row * experts, capacity, 1),
            ("erow", "ecol"),
            split_axis=0,
            concat_axis=0,
            tiled=True,
        ),
    )
    summed = jnp.einsum(
        "ts,rsd->trd",
        place_flat,
        returned.reshape(n_row, experts * capacity, weight_slice),
        preferred_element_type=jnp.float32,
    )
    slot_dprob = jnp.sum(
        returned_prob.astype(jnp.float32).reshape(n_row, experts, capacity), axis=0
    )
    return (summed.reshape(place_flat.shape[0], n_row * weight_slice), slot_dprob)


def reduce_parts(partial_term):
    return lax.psum(partial_term.astype(jnp.bfloat16), "erow").astype(jnp.float32)


def on_device(tokens, routes, gate_probs, cotangent, w_gate_up, w_down):
    n_row = lax.axis_size("erow")
    experts = lax.axis_size("ecol")
    token_count = tokens.shape[0]
    capacity = token_count // 2
    chosen = routes[:, :, None] == jnp.arange(experts, dtype=jnp.int32)[None, None, :]
    member = jnp.sum(chosen.astype(jnp.int32), axis=1)
    prior_result = jnp.cumsum(member, axis=0) - member
    placed = (member[:, :, None] == 1) & (
        prior_result[:, :, None] == jnp.arange(capacity, dtype=jnp.int32)[None, None, :]
    )
    placed = placed.astype(jnp.bfloat16)
    place_flat = placed.reshape(token_count, experts * capacity)
    probs_te = jnp.sum(
        jnp.where(chosen, gate_probs[:, :, None], jnp.zeros((), jnp.bfloat16)), axis=1
    )
    slot_probs = jnp.einsum(
        "tec,te->ec", placed, probs_te, preferred_element_type=jnp.float32
    ).astype(jnp.bfloat16)
    x_rows, cot_rows, prob_rows = send_rows(
        place_flat, slot_probs, tokens, cotangent, n_row, experts, capacity
    )
    prob_f32 = prob_rows.astype(jnp.float32)
    w_in = w_gate_up[0]
    w_out = w_down[0]
    partial_value = jnp.einsum("rd,dgf->rgf", x_rows, w_in, preferred_element_type=jnp.float32)
    pre_sums = reduce_parts(partial_value)
    gate_pre = pre_sums[:, 0, :]
    up_pre = pre_sums[:, 1, :]
    sigmoid_gate = jax.nn.sigmoid(gate_pre)
    activated = gate_pre * sigmoid_gate
    hidden = (activated * up_pre).astype(jnp.bfloat16)
    expert_out = jnp.dot(hidden, w_out, preferred_element_type=jnp.float32)
    contrib = (prob_f32[:, None] * expert_out).astype(jnp.bfloat16)
    layer_out = return_values(contrib, place_flat, n_row, experts, capacity).astype(jnp.bfloat16)
    cot_f32 = cot_rows.astype(jnp.float32)
    scaled_cotangent = (prob_f32[:, None] * cot_f32).astype(jnp.bfloat16)
    dprob_rows = jnp.sum(cot_f32 * expert_out, axis=1, keepdims=True).astype(jnp.bfloat16)
    hidden_term = jnp.einsum(
        "rd,fd->rf", scaled_cotangent, w_out, preferred_element_type=jnp.float32
    )
    hidden_gradient = reduce_parts(hidden_term[:, None, :])[:, 0, :]
    grad_gate = hidden_gradient * up_pre * sigmoid_gate * (1.0 + gate_pre * (1.0 - sigmoid_gate))
    grad_up = hidden_gradient * activated
    grad_pre = jnp.stack([grad_gate, grad_up], axis=1).astype(jnp.bfloat16)
    grad_rows = jnp.einsum(
        "rgf,dgf->rd", grad_pre, w_in, preferred_element_type=jnp.float32
    ).astype(jnp.bfloat16)
    grad_gate_up = jnp.einsum(
        "rd,rgf->dgf", x_rows, grad_pre, preferred_element_type=jnp.float32
    ).astype(jnp.bfloat16)[None]
    grad_down = jnp.einsum(
        "rf,rd->fd", hidden, scaled_cotangent, preferred_element_type=jnp.float32
    ).astype(jnp.bfloat16)[None]
    token_grads, slot_dprob = return_grads(
        grad_rows, dprob_rows, place_flat, n_row, experts, capacity
    )
    grad_tokens = token_grads.astype(jnp.bfloat16)
    dprob_te = jnp.sum(placed.astype(jnp.float32) * slot_dprob[None, :, :], axis=2)
    grad_probs = jnp.sum(jnp.where(chosen, dprob_te[:, None, :], 0.0), axis=2)
    return (layer_out, grad_tokens, grad_probs, grad_gate_up, grad_down)


def solution(mesh):
    placed = (
        P(("erow", "ecol"), None),
        P(("erow", "ecol"), None),
        P(("erow", "ecol"), None),
        P(("erow", "ecol"), None),
        P("ecol", "erow", None, None),
        P("ecol", None, "erow"),
    )
    return jax.shard_map(
        on_device,
        mesh=mesh,
        in_specs=placed,
        out_specs=(
            P(("erow", "ecol"), None),
            P(("erow", "ecol"), None),
            P(("erow", "ecol"), None),
            P("ecol", "erow", None, None),
            P("ecol", None, "erow"),
        ),
        check_vma=False,
    )
```

profile of v0, /device:TPU:1, one launch (start us, length us, event | category | flops | bytes accessed | tf_op | source)
XLA Modules:
  0.0 272.2 jit_solution(8297576986876873763)
XLA Ops:
  10.1 11.5 %all-to-all-start = ((bf16[128,4,1]{1,2,0:T(2,128)(2,1)}), bf16[128,4,1]{1,2,0:T(2,128)(2,1)S(1)}, u32[]{:S(2)}, u32[]{:S(2)}) async-start(bf16[128,4,1]{1,2,0:T(2,128)(2,1)} %copy.83), calls=%async_computation | async-start | bytes 131072 | tf_op jit(solution)/shard_map/all_to_all | solution.py:28
  23.2 8.2 %all-to-all-done = bf16[128,4,1]{1,2,0:T(2,128)(2,1)S(1)} async-done(((bf16[128,4,1]{1,2,0:T(2,128)(2,1)}), bf16[128,4,1]{1,2,0:T(2,128)(2,1)S(1)}, u32[]{:S(2)}, u32[]{:S(2)}) %all-to-all-start) | async-done | bytes 1056 | tf_op jit(solution)/shard_map/all_to_all | solution.py:28
  31.4 4.3 %all-to-all-start.3 = ((bf16[128,4,896]{2,1,0:T(4,128)(2,1)}), bf16[128,4,896]{2,1,0:T(4,128)(2,1)S(1)}, u32[]{:S(2)}, u32[]{:S(2)}) async-start(bf16[128,4,896]{2,1,0:T(4,128)(2,1)} %reshape.229), calls=%async_computation.3 | async-start | bytes 1835008 | tf_op jit(solution)/shard_map/all_to_all | solution.py:27
  37.2 16.1 %all-to-all-done.3 = bf16[128,4,896]{2,1,0:T(4,128)(2,1)S(1)} async-done(((bf16[128,4,896]{2,1,0:T(4,128)(2,1)}), bf16[128,4,896]{2,1,0:T(4,128)(2,1)S(1)}, u32[]{:S(2)}, u32[]{:S(2)}) %all-to-all-start.3) | async-done | bytes 917536 | tf_op jit(solution)/shard_map/all_to_all | solution.py:27
  53.3 4.6 %all-to-all-start.1 = ((bf16[128,4,896]{2,1,0:T(4,128)(2,1)}), bf16[128,4,896]{2,1,0:T(4,128)(2,1)S(1)}, u32[]{:S(2)}, u32[]{:S(2)}) async-start(bf16[128,4,896]{2,1,0:T(4,128)(2,1)} %reshape.224), calls=%async_computation.1 | async-start | bytes 1835008 | tf_op jit(solution)/shard_map/all_to_all | solution.py:26
  59.8 6.0 %fusion.19 = bf16[512,1,2048]{2,0,1:T(8,128)(2,1)} fusion(bf16[512,896]{1,0:T(8,128)(2,1)} %convert_element_type.134, bf16[1,2048,896]{2,1,0:T(8,128)(2,1)} %param.11), kind=kOutput, calls=%fused_computation.24 | convolution fusion | flops 1880096768 | bytes 6684672 | tf_op jit(solution)/shard_map/rd,fd->rf/dot_general | solution.py:123
  65.9 9.8 %all-to-all-done.1 = bf16[128,4,896]{2,1,0:T(4,128)(2,1)S(1)} async-done(((bf16[128,4,896]{2,1,0:T(4,128)(2,1)}), bf16[128,4,896]{2,1,0:T(4,128)(2,1)S(1)}, u32[]{:S(2)}, u32[]{:S(2)}) %all-to-all-start.1) | async-done | bytes 917536 | tf_op jit(solution)/shard_map/all_to_all | solution.py:26
  75.8 14.2 %fusion.9 = bf16[512,2,2048]{2,0,1:T(8,128)(2,1)} fusion(bf16[512,896,1]{1,0,2:T(8,128)(2,1)S(1)} %reshape.242, bf16[896,2,2048]{2,1,0:T(2,128)(2,1)} %bitcast.74), kind=kOutput, calls=%fused_computation.17 | convolution fusion | flops 3760193536 | bytes 12451840 | tf_op jit(solution)/shard_map/rd,dgf->rgf/dot_general | solution.py:110
  91.7 78.4 %all-reduce.3.cloned.1.call-done = (bf16[512,2,2048]{2,0,1:T(8,128)(2,1)}, bf16[512,1,2048]{2,0,1:T(8,128)(2,1)}) async-done(((bf16[512,2,2048]{2,0,1:T(8,128)(2,1)}, bf16[512,1,2048]{2,0,1:T(8,128)(2,1)}), (bf16[512,2,2048]{2,0,1:T(8,128)(2,1)}, bf16[512,1,2048]{2,0,1:T(8,128)(2,1)})) %all-reduce.3.cloned.1.call-update) | async-done | bytes 6291472 | tf_op jit(solution)/shard_map/psum | solution.py:82
  170.1 3.4 %convert_element_type.123 = f32[512,2,2048]{2,0,1:T(8,128)S(1)} convert(bf16[512,2,2048]{2,0,1:T(8,128)(2,1)} %get-tuple-element.40) | non-fusion elementwise | flops 2097152 | bytes 12582912 | tf_op jit(solution)/shard_map/convert_element_type | solution.py:82
  173.6 4.2 %fusion.6 = (bf16[512,1,2048]{2,0,1:T(8,128)(2,1)S(1)}, bf16[512,1,2048]{2,0,1:T(8,128)(2,1)}, bf16[512,2048]{1,0:T(8,128)(2,1)S(1)}) fusion(bf16[512,1,2048]{2,0,1:T(8,128)(2,1)S(1)} %copy-done.5, f32[512,2,2048]{2,0,1:T(8,128)S(1)} %convert_element_type.123), kind=kLoop, calls=%fused_computation.11 | loop fusion | flops 16777216 | bytes 16777216 | tf_op jit(solution)/shard_map/convert.5
  177.7 3.3 %multiply_reduce_fusion = (bf16[512]{0:T(512)(128)(2,1)S(1)}, bf16[512,896]{1,0:T(8,128)(2,1)}) fusion(f32[512,896]{1,0:T(8,128)S(1)} %copy-done.6, f32[512]{0:T(512)S(1)} %reshape.234, bf16[512,2048]{1,0:T(8,128)(2,1)S(1)} %get-tuple-element.46, bf16[1,2048,896]{2,1,0:T(8,128)(2,1)S(1)} %copy-done.10), kind=kOutput, calls=%fused_computation.27 | convolution fusion | flops 1880882688 | bytes 8522752 | tf_op jit(solution)/shard_map/dot_general | solution.py:117
  181.8 8.4 %all-to-all-start.5 = ((bf16[128,4,1]{1,2,0:T(2,128)(2,1)}), bf16[128,4,1]{1,2,0:T(2,128)(2,1)S(1)}, u32[]{:S(2)}, u32[]{:S(2)}) async-start(bf16[128,4,1]{1,2,0:T(2,128)(2,1)} %convert_element_type.151), calls=%async_computation.5 | async-start | bytes 131072 | tf_op jit(solution)/shard_map/all_to_all | solution.py:61
  191.3 2.5 reshape.226
  193.9 6.0 %all-to-all-done.5 = bf16[128,4,1]{1,2,0:T(2,128)(2,1)S(1)} async-done(((bf16[128,4,1]{1,2,0:T(2,128)(2,1)}), bf16[128,4,1]{1,2,0:T(2,128)(2,1)S(1)}, u32[]{:S(2)}, u32[]{:S(2)}) %all-to-all-start.5) | async-done | bytes 1056 | tf_op jit(solution)/shard_map/all_to_all | solution.py:61
  199.9 4.3 %all-to-all-start.2 = ((bf16[128,4,896]{2,1,0:T(4,128)(2,1)}), bf16[128,4,896]{2,1,0:T(4,128)(2,1)S(1)}, u32[]{:S(2)}, u32[]{:S(2)}) async-start(bf16[128,4,896]{2,1,0:T(4,128)(2,1)} %reshape.226), calls=%async_computation.2 | async-start | bytes 1835008 | tf_op jit(solution)/shard_map/all_to_all | solution.py:35
  204.2 10.2 %bitcast_convert_fusion = bf16[512,896]{1,0:T(8,128)(2,1)} fusion(bf16[896,2,2048]{2,1,0:T(2,128)(2,1)} %bitcast.75, bf16[512,1,2048]{2,0,1:T(8,128)(2,1)} %get-tuple-element.45, bf16[512,1,2048]{2,0,1:T(8,128)(2,1)S(1)} %get-tuple-element.44), kind=kOutput, calls=%fused_computation.26 | convolution fusion | flops 3760652288 | bytes 12451840 | tf_op jit(solution)/shard_map/rgf,dgf->rd/dot_general | solution.py:130
  214.4 2.5 reshape.230
  217.0 4.9 %all-to-all-done.2 = bf16[128,4,896]{2,1,0:T(4,128)(2,1)S(1)} async-done(((bf16[128,4,896]{2,1,0:T(4,128)(2,1)}), bf16[128,4,896]{2,1,0:T(4,128)(2,1)S(1)}, u32[]{:S(2)}, u32[]{:S(2)}) %all-to-all-start.2) | async-done | bytes 917536 | tf_op jit(solution)/shard_map/all_to_all | solution.py:35
  221.8 5.0 %all-to-all-start.4 = ((bf16[128,4,896]{2,1,0:T(4,128)(2,1)}), bf16[128,4,896]{2,1,0:T(4,128)(2,1)S(1)}, u32[]{:S(2)}, u32[]{:S(2)}) async-start(bf16[128,4,896]{2,1,0:T(4,128)(2,1)} %reshape.230), calls=%async_computation.4 | async-start | bytes 1835008 | tf_op jit(solution)/shard_map/all_to_all | solution.py:54
  226.8 6.5 %convert_bitcast_fusion = bf16[1,896,2,2048]{3,1,2,0:T(8,128)(2,1)S(1)} fusion(bf16[512,1,2048]{2,0,1:T(8,128)(2,1)} %get-tuple-element.45, bf16[512,1,2048]{2,0,1:T(8,128)(2,1)} %copy-done.4, bf16[512,896]{1,0:T(8,128)(2,1)} %reshape.225), kind=kOutput, calls=%fused_computation.2 | convolution fusion | flops 3770155008 | bytes 12451840 | tf_op jit(solution)/shard_map/rd,rgf->dgf/dot_general | solution.py:133
  233.4 21.9 %copy.95 = bf16[1,896,2,2048]{3,2,1,0:T(2,128)(2,1)} copy(bf16[1,896,2,2048]{3,1,2,0:T(8,128)(2,1)S(1)} %convert_bitcast_fusion) | data formatting | bytes 14680064
  255.2 4.2 %convert_bitcast_fusion.1 = bf16[1,2048,896]{2,1,0:T(8,128)(2,1)} fusion(bf16[512,2048]{1,0:T(8,128)(2,1)S(1)} %copy-done.3, bf16[512,896]{1,0:T(8,128)(2,1)S(1)} %copy-done.7), kind=kOutput, calls=%fused_computation.22 | convolution fusion | flops 1880883200 | bytes 6684672 | tf_op jit(solution)/shard_map/rf,rd->fd/dot_general | solution.py:136
  262.3 2.1 convolution_convert_fusion.1
  (64 shorter events, 15.4 us)
Async XLA Ops:
  7.2 14.5 %copy-start = (bf16[8,7168]{1,0:T(8,128)(2,1)S(1)}, bf16[8,7168]{1,0:T(8,128)(2,1)}, u32[]{:S(2)}) copy-start(bf16[8,7168]{1,0:T(8,128)(2,1)} %param.9) | copy-start | bytes 344068
  7.2 28.5 %copy-start.8 = (bf16[8,7168]{1,0:T(8,128)(2,1)S(1)}, bf16[8,7168]{1,0:T(8,128)(2,1)}, u32[]{:S(2)}) copy-start(bf16[8,7168]{1,0:T(8,128)(2,1)} %param.6) | copy-start | bytes 344068
  10.1 21.2 %all-to-all-start = ((bf16[128,4,1]{1,2,0:T(2,128)(2,1)}), bf16[128,4,1]{1,2,0:T(2,128)(2,1)S(1)}, u32[]{:S(2)}, u32[]{:S(2)}) async-start(bf16[128,4,1]{1,2,0:T(2,128)(2,1)} %copy.83), calls=%async_computation | async-start | bytes 131072 | tf_op jit(solution)/shard_map/all_to_all | solution.py:28
  31.4 21.9 %all-to-all-start.3 = ((bf16[128,4,896]{2,1,0:T(4,128)(2,1)}), bf16[128,4,896]{2,1,0:T(4,128)(2,1)S(1)}, u32[]{:S(2)}, u32[]{:S(2)}) async-start(bf16[128,4,896]{2,1,0:T(4,128)(2,1)} %reshape.229), calls=%async_computation.3 | async-start | bytes 1835008 | tf_op jit(solution)/shard_map/all_to_all | solution.py:27
  53.3 22.3 %all-to-all-start.1 = ((bf16[128,4,896]{2,1,0:T(4,128)(2,1)}), bf16[128,4,896]{2,1,0:T(4,128)(2,1)S(1)}, u32[]{:S(2)}, u32[]{:S(2)}) async-start(bf16[128,4,896]{2,1,0:T(4,128)(2,1)} %reshape.224), calls=%async_computation.1 | async-start | bytes 1835008 | tf_op jit(solution)/shard_map/all_to_all | solution.py:26
  57.9 112.2 %all-reduce.3.cloned.1.call-start = ((), (), s32[]{:S(2)}) async-start(), calls=%async_computation.6 | async-start | bytes 12582912 | tf_op jit(solution)/shard_map/psum | solution.py:82
  170.1 3.4 %copy-start.5 = (bf16[512,1,2048]{2,0,1:T(8,128)(2,1)S(1)}, bf16[512,1,2048]{2,0,1:T(8,128)(2,1)}, u32[]{:S(2)}) copy-start(bf16[512,1,2048]{2,0,1:T(8,128)(2,1)} %get-tuple-element.41) | copy-start | bytes 6291460
  173.5 4.2 %copy-start.6 = (f32[512,896]{1,0:T(8,128)S(1)}, f32[512,896]{1,0:T(8,128)}, u32[]{:S(2)}) copy-start(f32[512,896]{1,0:T(8,128)} %reshape.236) | copy-start | bytes 5505028
  173.5 4.2 %copy-start.10 = (bf16[1,2048,896]{2,1,0:T(8,128)(2,1)S(1)}, bf16[1,2048,896]{2,1,0:T(8,128)(2,1)}, u32[]{:S(2)}) copy-start(bf16[1,2048,896]{2,1,0:T(8,128)(2,1)} %param.11) | copy-start | bytes 11010052
  177.7 3.3 %copy-start.2 = (bf16[512,2048]{1,0:T(8,128)(2,1)}, bf16[512,2048]{1,0:T(8,128)(2,1)S(1)}, u32[]{:S(2)}) copy-start(bf16[512,2048]{1,0:T(8,128)(2,1)S(1)} %get-tuple-element.46) | copy-start | bytes 6291460
  177.7 26.5 %copy-start.4 = (bf16[512,1,2048]{2,0,1:T(8,128)(2,1)}, bf16[512,1,2048]{2,0,1:T(8,128)(2,1)S(1)}, u32[]{:S(2)}) copy-start(bf16[512,1,2048]{2,0,1:T(8,128)(2,1)S(1)} %get-tuple-element.44) | copy-start | bytes 6291460
  181.8 18.1 %all-to-all-start.5 = ((bf16[128,4,1]{1,2,0:T(2,128)(2,1)}), bf16[128,4,1]{1,2,0:T(2,128)(2,1)S(1)}, u32[]{:S(2)}, u32[]{:S(2)}) async-start(bf16[128,4,1]{1,2,0:T(2,128)(2,1)} %convert_element_type.151), calls=%async_computation.5 | async-start | bytes 131072 | tf_op jit(solution)/shard_map/all_to_all | solution.py:61
  199.9 21.9 %all-to-all-start.2 = ((bf16[128,4,896]{2,1,0:T(4,128)(2,1)}), bf16[128,4,896]{2,1,0:T(4,128)(2,1)S(1)}, u32[]{:S(2)}, u32[]{:S(2)}) async-start(bf16[128,4,896]{2,1,0:T(4,128)(2,1)} %reshape.226), calls=%async_computation.2 | async-start | bytes 1835008 | tf_op jit(solution)/shard_map/all_to_all | solution.py:35
  221.8 40.1 %all-to-all-start.4 = ((bf16[128,4,896]{2,1,0:T(4,128)(2,1)}), bf16[128,4,896]{2,1,0:T(4,128)(2,1)S(1)}, u32[]{:S(2)}, u32[]{:S(2)}) async-start(bf16[128,4,896]{2,1,0:T(4,128)(2,1)} %reshape.230), calls=%async_computation.4 | async-start | bytes 1835008 | tf_op jit(solution)/shard_map/all_to_all | solution.py:54
  233.3 21.9 %copy-start.3 = (bf16[512,2048]{1,0:T(8,128)(2,1)S(1)}, bf16[512,2048]{1,0:T(8,128)(2,1)}, u32[]{:S(2)}) copy-start(bf16[512,2048]{1,0:T(8,128)(2,1)} %copy-done.2) | copy-start | bytes 6291460
  233.3 21.9 %copy-start.7 = (bf16[512,896]{1,0:T(8,128)(2,1)S(1)}, bf16[512,896]{1,0:T(8,128)(2,1)}, u32[]{:S(2)}) copy-start(bf16[512,896]{1,0:T(8,128)(2,1)} %convert_element_type.134) | copy-start | bytes 2752516
  255.2 4.7 %copy-start.9 = (s32[8,4]{0,1:T(4,128)S(1)}, s32[8,4]{0,1:T(4,128)}, u32[]{:S(2)}) copy-start(s32[8,4]{0,1:T(4,128)} %param.7) | copy-start | bytes 388
  260.7 4.7 %copy-start.1 = (bf16[8,7168]{1,0:T(8,128)(2,1)S(1)}, bf16[8,7168]{1,0:T(8,128)(2,1)}, u32[]{:S(2)}) copy-start(bf16[8,7168]{1,0:T(8,128)(2,1)} %param.9) | copy-start | bytes 344068
Sparse Core Ops, SparseCore 0:
  90.2 79.9 all-reduce.2
where the time goes:
time: 273 us; the launch traced here: 272 us
  waiting for transfers between devices  123 us (45%)
  matrix products  48.3 us (18%)
  starting transfers between devices  38.2 us (14%)
  local copies, waits for them, and re-layouts  37.2 us (14%)
  between operations  14.3 us (5%)
  other arithmetic  10.8 us (4%)
    psum x1, waiting for transfers between devices, reduce_parts(): lax.psum(partial_term.astype(jnp.bfloat16), 'erow').astype(jnp.float32)  78.4 us
    unnamed x24, local copies, waits for them, and re-layouts  22 us
    all_to_all x1, waiting for transfers between devices, send_rows(): lax.all_to_all(cot_out, ('erow', 'ecol'), split_axis=0, concat_axis=0, ti...  16.1 us
    dot_general x1, matrix products, on_device(): jnp.einsum('rd,dgf->rgf', x_rows, w_in, preferred_element_type=jnp.float32)  14.2 us
    all_to_all x1, starting transfers between devices, send_rows(): lax.all_to_all(prob_out, ('erow', 'ecol'), split_axis=0, concat_axis=0, t...  11.5 us
    dot_general x1, matrix products, on_device(): jnp.einsum('rgf,dgf->rd', grad_pre, w_in, preferred_element_type=jnp.floa...  10.2 us
    all_to_all x1, waiting for transfers between devices, send_rows(): lax.all_to_all(x_out, ('erow', 'ecol'), split_axis=0, concat_axis=0, tile...  9.75 us
    all_to_all x1, starting transfers between devices, return_grads(): lax.all_to_all(dprob_rows.reshape(n_row * experts, capacity, 1), ('erow',...  8.4 us
  transfers between devices with their start and end apart: 7, of which 6 were waited for; matrix products, arithmetic and copies ran while one was open for 23% of the time, Pallas kernels for 0%

commit v1 on v0

v1 whole, which is shorter than its diff:
```python
import jax
import jax.numpy as jnp
from jax import lax
from jax.experimental import pallas as pl
from jax.experimental.pallas import tpu as pltpu
from jax.sharding import PartitionSpec as P

BF = jnp.bfloat16
F32 = jnp.float32
MESH = pl.DeviceIdType.MESH
NX, NK, NZ, NY = 4, 2, 4, 4
NR, NE = NX * NK, NZ * NY
CAP = 4
NQ = 4
OFFSETS = (
    (0, 0), (0, 1), (0, 3), (1, 0),
    (2, 2), (1, 2), (2, 1), (1, 1),
    (3, 2), (2, 3), (3, 3), (2, 0),
    (3, 0), (1, 3), (3, 1), (0, 2),
)
BPQ = len(OFFSETS) // NQ
SCHEDULE = (
    "D0", "S0", "D1", "W0", "D2", "D3", "C0", "S1", "R0", "B0",
    "S2", "C1", "A0", "R1", "B1", "S3", "F0", "C2", "A1", "R2",
    "G0", "B2", "O0", "F1", "C3", "A2", "R3", "B3", "G1", "O1",
    "F2", "A3", "G2", "O2", "F3", "K0", "G3", "O3", "K1", "K2",
    "K3",
)


def dot(a, b):
    return jnp.dot(a, b, preferred_element_type=F32)


def dot_nt(a, b):
    return lax.dot_general(a, b, (((1,), (1,)), ((), ())), preferred_element_type=F32)


def dot_tn(a, b):
    return lax.dot_general(a, b, (((0,), (0,)), ((), ())), preferred_element_type=F32)


def layer_kernel(
    tok, cot, routes, probs, wgu_hbm, wd_hbm,
    lay_out, gtok_out, dp_out, rows_hbm, act_hbm,
    xb, tb, selp, selq, sb, xr, stg, wgu, wd, pa, cr, own, dep, s2, sn, sd, m1, m2, ga,
    oacc, ob, rr, lacc, dacc, fb, fr,
    w_sem, s1_s, s1_r, s2_s, s2_r, loc, ce_s, ce_r, m1_s, m1_r, n_s, n_r, m2_s, m2_r, ag_s, ag_r,
    rt_s, rt_r, fx_s, fx_r, hb,
):
    er = lax.axis_index("erow")
    ec = lax.axis_index("ecol")
    x, k = er // NK, er % NK
    z, y = ec // NY, ec % NY
    wdt = wd.shape[1]
    fs = wgu.shape[2] // 2
    half = xr.shape[1] * BPQ // 2
    rows = xr.shape[1] * BPQ

    def row_at(dx, dk):
        return {"erow": ((x + dx) % NX) * NK + (k + dk) % NK}

    def col_at(dz, dy):
        return {"ecol": ((z + dz) % NZ) * NY + (y + dy) % NY}

    def remote(src, dst, ss, rs, dev):
        return pltpu.make_async_remote_copy(
            src_ref=src, dst_ref=dst, send_sem=ss, recv_sem=rs, device_id=dev, device_id_type=MESH
        )

    wd_copy = pltpu.make_async_copy(wd_hbm.at[0], wd, w_sem.at[16])

    def w_copy(c):
        return pltpu.make_async_copy(
            wgu_hbm.at[0, :, :, pl.ds(pl.multiple_of(c * 128, 128), 128)], stg.at[c], w_sem.at[c]
        )

    for c in range(16):
        w_copy(c).start()
    wd_copy.start()

    bar = pltpu.get_barrier_semaphore()
    for d in range(1, NR):
        pl.semaphore_signal(bar, inc=1, device_id=row_at(d // NK, d % NK), device_id_type=MESH)
    for dz, dy in OFFSETS[1:]:
        pl.semaphore_signal(bar, inc=1, device_id=col_at(dz, dy), device_id_type=MESH)

    lane = lax.broadcasted_iota(jnp.int32, (8, 128), 1)
    row8 = lax.broadcasted_iota(jnp.int32, (8, 128), 0)
    expert = (lane % (NE * CAP)) // CAP
    member = jnp.zeros((8, 128), F32)
    weight = jnp.zeros((8, 128), F32)
    eye = jnp.where(
        lax.broadcasted_iota(jnp.int32, (8, 8), 0) == lax.broadcasted_iota(jnp.int32, (8, 8), 1), 1.0, 0.0
    ).astype(BF)
    rt = dot_nt(eye, routes[...].astype(F32).astype(BF))
    gp = dot_nt(eye, probs[...])
    for j in range(rt.shape[1]):
        hit = rt[:, j : j + 1] == expert.astype(F32)
        member = member + jnp.where(hit, 1.0, 0.0)
        weight = weight + jnp.where(hit, gp[:, j : j + 1], 0.0)
    prior = jnp.zeros((8, 128), F32)
    for t in range(7):
        prior = prior + jnp.where(row8 > t, member[t : t + 1, :], 0.0)
    place = jnp.where(prior == (lane % CAP).astype(F32), member, 0.0)
    meta = jnp.where(lane < NE * CAP, place, place * weight).astype(BF)

    def block_of(ref, r):
        return ref[:, pl.ds(pl.multiple_of(r * wdt, 128), wdt)]

    for d in range(NR):
        dst = xb if d else tb
        r = ((x + d // NK) % NX) * NK + (k + d % NK) % NK
        dst[d, :, 0:wdt] = block_of(tok, r)
        dst[d, :, wdt : 2 * wdt] = block_of(cot, r)
        dst[d, :, 2 * wdt :] = meta

    pl.semaphore_wait(bar, NR - 1 + NE - 1)

    first = []
    for d in range(1, NR):
        cp = remote(xb.at[d], tb.at[d], s1_s.at[d], s1_r.at[d], row_at(d // NK, d % NK))
        cp.start()
        first.append(cp)

    pi = lax.broadcasted_iota(jnp.int32, (256, 256), 0)
    pj = lax.broadcasted_iota(jnp.int32, (256, 256), 1)
    perm = jnp.where(pj == jnp.where(pi < 128, 2 * pi, 2 * pi - 255), 1.0, 0.0).astype(BF)

    def spread(c, carry):
        w_copy(c).wait()
        raw = stg.at[c].reshape(2 * wdt, 128)
        s, h = c // 2, c % 2
        for b in range(wdt // 128):
            v = dot(perm, raw[pl.ds(b * 256, 256), :]).astype(BF)
            wgu[s, b * 128 : (b + 1) * 128, pl.ds(pl.multiple_of(h * 128, 128), 128)] = v[:128]
            wgu[s, b * 128 : (b + 1) * 128, pl.ds(pl.multiple_of(fs + h * 128, 128), 128)] = v[128:]
        return carry

    lax.fori_loop(0, 6, spread, 0)

    for cp in first:
        cp.wait_recv()

    def sender(d):
        return ((x + NX - d // NK) % NX) * NK + (k + d) % NK

    t_all = tb[...].reshape(NR * 8, 2 * wdt + 128)
    x_all = t_all[:, 0:wdt]
    c_all = t_all[:, wdt : 2 * wdt]
    m_all = t_all[:, 2 * wdt :]
    si = lax.broadcasted_iota(jnp.int32, (rows, 128), 0)
    mi = lax.broadcasted_iota(jnp.int32, (rows, 128), 1)
    second = {}

    def stage_d(q):
        want = jnp.zeros((rows, 128), jnp.int32)
        for b in range(BPQ):
            dz, dy = OFFSETS[q * BPQ + b]
            e = ((z + dz) % NZ) * NY + (y + dy) % NY
            want = jnp.where(si // 32 == b, e, want)
        match = ((mi % (NE * CAP)) // CAP == want) & (mi % CAP == si % CAP)
        e_hot = jnp.where(match & (mi < NE * CAP), 1.0, 0.0).astype(BF)
        e_wgt = jnp.where(match & (mi >= NE * CAP), 1.0, 0.0).astype(BF)
        ti = lax.broadcasted_iota(jnp.int32, (rows, NR * 8), 1)
        sj = lax.broadcasted_iota(jnp.int32, (rows, NR * 8), 0)
        mine = (sj % 32) // CAP == sender(ti // 8)
        hot_t = jnp.where(mine, dot_nt(e_hot, m_all), 0.0).astype(BF)
        wgt_t = jnp.where(mine, dot_nt(e_wgt, m_all), 0.0).astype(BF)
        ti2 = lax.broadcasted_iota(jnp.int32, (NR * 8, rows), 0)
        sj2 = lax.broadcasted_iota(jnp.int32, (NR * 8, rows), 1)
        mine2 = (sj2 % 32) // CAP == sender(ti2 // 8)
        selq[q] = jnp.where(mine2, dot_nt(m_all, e_hot), 0.0).astype(BF)
        selp[q] = jnp.where(mine2, dot_nt(m_all, e_wgt), 0.0).astype(BF)
        xs = dot(hot_t, x_all).astype(BF).reshape(BPQ, 32, wdt)
        cs = dot(wgt_t, c_all).astype(BF).reshape(BPQ, 32, wdt)
        sb[q * BPQ : (q + 1) * BPQ, :, 0:wdt] = xs
        sb[q * BPQ : (q + 1) * BPQ, :, wdt:] = cs

    def stage_s(q):
        for i in range(q * BPQ, (q + 1) * BPQ):
            if i == 0:
                cp = pltpu.make_async_copy(sb.at[0], xr.at[0], loc.at[0])
            else:
                cp = remote(sb.at[i], xr.at[i], s2_s.at[i], s2_r.at[i], col_at(*OFFSETS[i]))
            cp.start()
            second[i] = cp

    def stage_w(half_of):
        if half_of == 0:
            lax.fori_loop(6, 16, spread, 0)
            wd_copy.wait()

    def slice_at(dx, dk):
        return ((x + dx) % NX) * NK + (k + dk) % NK

    def chunk(ref, q, lo, hi):
        return ref[q * BPQ : (q + 1) * BPQ, :, lo:hi].reshape(rows, hi - lo)

    copies = {}
    flying = []

    def send(name, *args):
        cp = remote(*args)
        cp.start()
        copies[name] = cp
        flying.append(cp)

    def partials(q, s):
        pre = dot(chunk(xr, q, 0, wdt), wgu[s])
        hg = dot_nt(chunk(xr, q, wdt, 2 * wdt), wd[pl.ds(pl.multiple_of(s * fs, fs), fs), :])
        return pre, hg

    def partial_to_partner(q, j, dx):
        pre, hg = partials(q, slice_at(dx, 1))
        pa[q, j, :, 0 : 2 * fs] = pre.astype(BF)
        pa[q, j, :, 2 * fs :] = hg.astype(BF)
        send(("ce", q, j), pa.at[q, j], cr.at[q, j], ce_s.at[q, j], ce_r.at[q, j], row_at(0, 1))

    def partial_sum(q, j, dx):
        pre, hg = partials(q, slice_at(dx, 0))
        copies["ce", q, j].wait_recv()
        return jnp.concatenate([pre, hg], axis=1) + cr[q, j].astype(F32)

    def stage_c(q):
        for i in range(q * BPQ, (q + 1) * BPQ):
            if i == 0:
                second[i].wait()
            else:
                second[i].wait_recv()
        for j, dx in enumerate((2, 1, 3)):
            partial_to_partner(q, j, dx)
        r2 = partial_sum(q, 0, 2)
        s2[q, 0] = r2[0:half].astype(BF)
        send(("m1", q, 0), s2.at[q, 0], m1.at[q, 0], m1_s.at[q, 0], m1_r.at[q, 0], row_at(1, 0))
        s2[q, 1] = r2[half:rows].astype(BF)
        send(("m1", q, 1), s2.at[q, 1], m1.at[q, 1], m1_s.at[q, 1], m1_r.at[q, 1], row_at(3, 0))
        r1 = partial_sum(q, 1, 1)
        sn[q, 0] = r1[half:rows].astype(BF)
        send(("n", q, 0), sn.at[q, 0], m2.at[q, 0, 1], n_s.at[q, 0], n_r.at[q, 0], row_at(1, 0))
        dep[q, 0] = r1[0:half]
        r3 = partial_sum(q, 2, 3)
        sn[q, 1] = r3[0:half].astype(BF)
        send(("n", q, 1), sn.at[q, 1], m2.at[q, 1, 0], n_s.at[q, 1], n_r.at[q, 1], row_at(3, 0))
        dep[q, 1] = r3[half:rows]

    def stage_b(q):
        partial_to_partner(q, 3, 0)
        own[q] = partial_sum(q, 3, 0)

    def stage_r(q):
        copies["m1", q, 0].wait_recv()
        sd[q, 0] = (dep[q, 0] + m1[q, 0].astype(F32)).astype(BF)
        send(("m2", q, 0), sd.at[q, 0], m2.at[q, 0, 0], m2_s.at[q, 0], m2_r.at[q, 0], row_at(1, 0))
        copies["m1", q, 1].wait_recv()
        sd[q, 1] = (dep[q, 1] + m1[q, 1].astype(F32)).astype(BF)
        send(("m2", q, 1), sd.at[q, 1], m2.at[q, 1, 1], m2_s.at[q, 1], m2_r.at[q, 1], row_at(3, 0))

    def stage_a(q):
        for d in range(2):
            copies["n", q, d].wait_recv()
            copies["m2", q, d].wait_recv()
        for h in range(2):
            lo, hi = h * half, (h + 1) * half
            tot = own[q, lo:hi, :] + m2[q, 0, h].astype(F32) + m2[q, 1, h].astype(F32)
            g, u, hg = tot[:, 0:fs], tot[:, fs : 2 * fs], tot[:, 2 * fs :]
            s = 1.0 / (1.0 + jnp.exp(-g))
            a = g * s
            ga[q, 0, lo:hi, 0:fs] = (a * u).astype(BF)
            ga[q, 0, lo:hi, fs : 2 * fs] = (hg * u * s * (1.0 + g * (1.0 - s))).astype(BF)
            ga[q, 0, lo:hi, 2 * fs :] = (hg * a).astype(BF)
        src = ga.at[q, 0]
        send(("ag", q, 0), src, ga.at[q, 2], ag_s.at[q, 0], ag_r.at[q, 0], row_at(1, 0))
        send(("ag", q, 1), src, ga.at[q, 6], ag_s.at[q, 1], ag_r.at[q, 1], row_at(3, 0))
        send(("ag", q, 2), src, ga.at[q, 1], ag_s.at[q, 2], ag_r.at[q, 2], row_at(0, 1))

    def stage_f(q):
        copies["ag", q, 0].wait_recv()
        send(("ag", q, 3), ga.at[q, 2, 0:half], ga.at[q, 4, 0:half], ag_s.at[q, 3], ag_r.at[q, 3], row_at(1, 0))
        send(("ag", q, 4), ga.at[q, 2], ga.at[q, 3], ag_s.at[q, 4], ag_r.at[q, 4], row_at(0, 1))
        copies["ag", q, 1].wait_recv()
        send(
            ("ag", q, 5), ga.at[q, 6, half:rows], ga.at[q, 4, half:rows], ag_s.at[q, 5], ag_r.at[q, 5], row_at(3, 0)
        )
        send(("ag", q, 6), ga.at[q, 6], ga.at[q, 7], ag_s.at[q, 6], ag_r.at[q, 6], row_at(0, 1))

    def stage_g(q):
        copies["ag", q, 3].wait_recv()
        copies["ag", q, 5].wait_recv()
        send(("ag", q, 7), ga.at[q, 4], ga.at[q, 5], ag_s.at[q, 7], ag_r.at[q, 7], row_at(0, 1))

    stores = []

    def stage_o(q):
        for j in (2, 4, 6, 7):
            copies["ag", q, j].wait_recv()
        for j in range(NR):
            s = slice_at(NX - j // NK, j % NK)
            cp = pltpu.make_async_copy(ga.at[q, j], act_hbm.at[s, pl.ds(q * rows, rows)], hb.at[q * NR + j])
            cp.start()
            stores.append(cp)

        def term(dx):
            s0, s1 = slice_at(NX - dx, 0), slice_at(NX - dx, 1)
            p0, p1 = ga[q, 2 * dx], ga[q, 2 * dx + 1]
            w0 = wd[pl.ds(pl.multiple_of(s0 * fs, fs), fs), :]
            w1 = wd[pl.ds(pl.multiple_of(s1 * fs, fs), fs), :]
            out = dot(p0[:, 0:fs], w0) + dot(p1[:, 0:fs], w1)
            grad = dot_nt(p0[:, fs:], wgu[s0]) + dot_nt(p1[:, fs:], wgu[s1])
            return out, grad

        out, grad = term(0)
        oacc[:, 0:wdt] = out
        oacc[:, wdt:] = grad

        def more(dx, carry):
            out, grad = term(dx)
            oacc[:, 0:wdt] += out
            oacc[:, wdt:] += grad
            return carry

        lax.fori_loop(1, NX, more, 0)
        ob[q * BPQ : (q + 1) * BPQ] = oacc[...].astype(BF).reshape(BPQ, 32, 2 * wdt)
        for i in range(q * BPQ, (q + 1) * BPQ):
            if i == 0:
                cp = pltpu.make_async_copy(ob.at[0], rr.at[0], loc.at[1])
                cp.start()
                copies["rt", 0] = cp
            else:
                dz, dy = OFFSETS[i]
                send(("rt", i), ob.at[i], rr.at[i], rt_s.at[i], rt_r.at[i], col_at(NZ - dz, NY - dy))

    def stage_k(q):
        for i in range(q * BPQ, (q + 1) * BPQ):
            if i == 0:
                copies["rt", 0].wait()
            else:
                copies["rt", i].wait_recv()
        eo = chunk(rr, q, 0, wdt)
        gr = chunk(rr, q, wdt, 2 * wdt)
        hot = selq[q]
        lay = dot(selp[q], eo)
        gt = dot(hot, gr)
        dots = dot_nt(tb[...].reshape(NR * 8, 2 * wdt + 128)[:, wdt : 2 * wdt], eo) * hot.astype(F32)
        li = lax.broadcasted_iota(jnp.int32, (NR * 8, 128), 1)
        dp = jnp.zeros((NR * 8, 128), F32)
        for b in range(BPQ):
            dz, dy = OFFSETS[q * BPQ + b]
            e = ((z + dz) % NZ) * NY + (y + dy) % NY
            total = jnp.sum(jnp.where(li // 32 == b, dots, 0.0), axis=1, keepdims=True)
            dp = dp + jnp.where(li == e, total, 0.0)
        if q == 0:
            lacc[:, 0:wdt] = lay
            lacc[:, wdt:] = gt
            dacc[...] = dp
        else:
            lacc[:, 0:wdt] += lay
            lacc[:, wdt:] += gt
            dacc[...] += dp

    stages = {"D": stage_d, "S": stage_s, "W": stage_w, "C": stage_c, "B": stage_b, "R": stage_r, "A": stage_a, "F": stage_f, "G": stage_g, "O": stage_o, "K": stage_k}
    for step in SCHEDULE:
        stages[step[0]](int(step[1:]))
        if step == "C3":
            cp = pltpu.make_async_copy(xr, rows_hbm, hb.at[NQ * NR])
            cp.start()
            stores.append(cp)

    for d in range(NR):
        dst = fb if d else fr
        dst[d, :, 0 : 2 * wdt] = lacc[d * 8 : (d + 1) * 8, :].astype(BF)
        dst[d, :, 2 * wdt :] = dacc[d * 8 : (d + 1) * 8, :].astype(BF)
    last = []
    for d in range(1, NR):
        cp = remote(fb.at[d], fr.at[d], fx_s.at[d], fx_r.at[d], row_at(NX - d // NK, d % NK))
        cp.start()
        last.append(cp)

    for cp in first:
        cp.wait_send()
    for i in range(1, NE):
        second[i].wait_send()
    for cp in flying:
        cp.wait_send()
    for cp in stores:
        cp.wait()

    total = jnp.zeros((8, 128), F32)
    for d in range(NR):
        if d:
            last[d - 1].wait_recv()
        r = slice_at(d // NK, d % NK)
        cols = pl.ds(pl.multiple_of(r * wdt, 128), wdt)
        lay_out[:, cols] = fr[d, :, 0:wdt]
        gtok_out[:, cols] = fr[d, :, wdt : 2 * wdt]
        total = total + fr[d, :, 2 * wdt :].astype(F32)
    picked = jnp.zeros((8, 128), F32)
    for j in range(rt.shape[1]):
        val = jnp.sum(jnp.where(rt[:, j : j + 1] == lane.astype(F32), total, 0.0), axis=1, keepdims=True)
        picked = picked + jnp.where(lane == j, val, 0.0)
    dp_out[...] = picked.T[0 : rt.shape[1], :]
    for cp in last:
        cp.wait_send()


def layer(tokens, cotangent, routes, gate_probs, w_gate_up, w_down):
    width = w_gate_up.shape[1]
    hid = w_gate_up.shape[3]
    fs = hid // NR
    tok = tokens.shape[0]
    blk = NR * CAP
    rows = BPQ * blk
    vm = pltpu.VMEM
    dma = pltpu.SemaphoreType.DMA
    scratch = [
        vm((NR, tok, 2 * width + 128), BF),
        vm((NR, tok, 2 * width + 128), BF),
        vm((NQ, NR * tok, rows), BF),
        vm((NQ, NR * tok, rows), BF),
        vm((NE, blk, 2 * width), BF),
        vm((NE, blk, 2 * width), BF),
        vm((hid // 128, width, 2, 128), BF),
        vm((NR, width, 2 * fs), BF),
        vm((hid, width), BF),
        vm((NQ, NX, rows, 3 * fs), BF),
        vm((NQ, NX, rows, 3 * fs), BF),
        vm((NQ, rows, 3 * fs), F32),
        vm((NQ, 2, rows // 2, 3 * fs), F32),
        vm((NQ, 2, rows // 2, 3 * fs), BF),
        vm((NQ, 2, rows // 2, 3 * fs), BF),
        vm((NQ, 2, rows // 2, 3 * fs), BF),
        vm((NQ, 2, rows // 2, 3 * fs), BF),
        vm((NQ, 2, 2, rows // 2, 3 * fs), BF),
        vm((NQ, NR, rows, 3 * fs), BF),
        vm((rows, 2 * width), F32),
        vm((NE, blk, 2 * width), BF),
        vm((NE, blk, 2 * width), BF),
        vm((NR * tok, 2 * width), F32),
        vm((NR * tok, 128), F32),
        vm((NR, tok, 2 * width + 128), BF),
        vm((NR, tok, 2 * width + 128), BF),
        dma((17,)),
        dma((NR,)), dma((NR,)),
        dma((NE,)), dma((NE,)),
        dma((2,)),
        dma((NQ, NX)), dma((NQ, NX)),
        dma((NQ, 2)), dma((NQ, 2)),
        dma((NQ, 2)), dma((NQ, 2)),
        dma((NQ, 2)), dma((NQ, 2)),
        dma((NQ, NR)), dma((NQ, NR)),
        dma((NE,)), dma((NE,)),
        dma((NR,)), dma((NR,)),
        dma((NQ * NR + 1,)),
    ]
    vmem = pl.BlockSpec(memory_space=pltpu.VMEM)
    hbm = pl.BlockSpec(memory_space=pl.ANY)
    return pl.pallas_call(
        layer_kernel,
        name="layer",
        out_shape=(
            jax.ShapeDtypeStruct(tokens.shape, BF),
            jax.ShapeDtypeStruct(tokens.shape, BF),
            jax.ShapeDtypeStruct(routes.shape, F32),
            jax.ShapeDtypeStruct((NE, blk, 2 * width), BF),
            jax.ShapeDtypeStruct((NR, NQ * rows, 3 * fs), BF),
        ),
        in_specs=[vmem, vmem, vmem, vmem, hbm, hbm],
        out_specs=(vmem, vmem, vmem, hbm, hbm),
        scratch_shapes=scratch,
        compiler_params=pltpu.CompilerParams(
            collective_id=0, has_side_effects=True, vmem_limit_bytes=60 << 20
        ),
    )(tokens, cotangent, routes, gate_probs, w_gate_up, w_down)


def grads_kernel(rows_ref, act_ref, a_ref, b_ref, c_ref, gd_ref, ggu_hbm, a_out, b_out, c_out, xt, stg, sem):
    s = pl.program_id(0)
    slot = s % 2
    width = rows_ref.shape[1] // 2
    fs = gd_ref.shape[1]

    def out_copy(step, h):
        c = step * 2 + h
        return pltpu.make_async_copy(
            stg.at[step % 2, h],
            ggu_hbm.at[0, :, :, pl.ds(pl.multiple_of(c * 128, 128), 128)],
            sem.at[step % 2, h],
        )

    @pl.when(s >= 2)
    def _():
        for h in range(2):
            out_copy(s - 2, h).wait()

    @pl.when(s == 0)
    def _():
        a_out[...] = a_ref[...]
        b_out[...] = b_ref[...]
        c_out[...] = c_ref[...]
        xt[...] = rows_ref[:, 0:width].T

    act = act_ref[0]
    gd_ref[0] = dot_tn(act[:, 0:fs], rows_ref[:, width:]).astype(BF)
    pi = lax.broadcasted_iota(jnp.int32, (256, 256), 0)
    pj = lax.broadcasted_iota(jnp.int32, (256, 256), 1)
    perm = jnp.where(pi == jnp.where(pj < 128, 2 * pj, 2 * pj - 255), 1.0, 0.0).astype(BF)
    g = dot(xt[...], act[:, fs:]).astype(BF)
    for b in range(width // 128):
        gb = g[b * 128 : (b + 1) * 128]
        v = dot(perm, jnp.concatenate([gb[:, 0:fs], gb[:, fs:]], axis=0)).astype(BF)
        for h in range(2):
            stg.at[slot, h].reshape(2 * width, 128)[pl.ds(b * 256, 256), :] = v[:, h * 128 : (h + 1) * 128]
    for h in range(2):
        out_copy(s, h).start()

    @pl.when(s == pl.num_programs(0) - 1)
    def _():
        for h in range(2):
            out_copy(s - 1, h).wait()
        for h in range(2):
            out_copy(s, h).wait()


def weight_grads(rows, act, small, width, hid):
    fs = hid // NR
    n = rows.shape[0]
    return pl.pallas_call(
        grads_kernel,
        name="weight_grads",
        grid=(NR,),
        out_shape=(
            jax.ShapeDtypeStruct((1, hid, width), BF),
            jax.ShapeDtypeStruct((1, width, 2, hid), BF),
            *(jax.ShapeDtypeStruct(v.shape, v.dtype) for v in small),
        ),
        in_specs=[
            pl.BlockSpec((n, 2 * width), lambda s: (0, 0)),
            pl.BlockSpec((1, n, 3 * fs), lambda s: (s, 0, 0)),
            *(pl.BlockSpec(v.shape, lambda s: (0, 0)) for v in small),
        ],
        out_specs=(
            pl.BlockSpec((1, fs, width), lambda s: (0, s, 0)),
            pl.BlockSpec(memory_space=pl.ANY),
            *(pl.BlockSpec(v.shape, lambda s: (0, 0)) for v in small),
        ),
        scratch_shapes=[
            pltpu.VMEM((width, n), BF),
            pltpu.VMEM((2, 2, width, 2, 128), BF),
            pltpu.SemaphoreType.DMA((2, 2)),
        ],
        compiler_params=pltpu.CompilerParams(vmem_limit_bytes=60 << 20),
    )(rows, act, *small)


def on_device(tokens, routes, gate_probs, cotangent, w_gate_up, w_down):
    width, hid = w_gate_up.shape[1], w_gate_up.shape[3]
    layer_out, grad_tokens, dprob, rows, act = layer(
        tokens, cotangent, routes.T, gate_probs.T, w_gate_up, w_down
    )
    grad_down, grad_gate_up, layer_out, grad_tokens, dprob = weight_grads(
        rows.reshape(-1, 2 * width), act, (layer_out, grad_tokens, dprob), width, hid
    )
    return (layer_out, grad_tokens, dprob.T, grad_gate_up, grad_down)


def solution(mesh):
    rows = P(("erow", "ecol"), None)
    up, down = P("ecol", "erow", None, None), P("ecol", None, "erow")
    return jax.shard_map(
        on_device,
        mesh=mesh,
        in_specs=(rows, rows, rows, rows, up, down),
        out_specs=(rows, rows, rows, up, down),
        check_vma=False,
    )
```

time: 273 us -> 132 us (0.48)
  Pallas kernels: 0 us -> 131 us
  waiting for transfers between devices: 123 us -> 0 us
  matrix products: 48.3 us -> 0 us
  starting transfers between devices: 38.2 us -> 0 us
  local copies, waits for them, and re-layouts: 37.2 us -> 0 us
  between operations: 14.3 us -> 0.8 us
  other arithmetic: 10.8 us -> 0 us
    pallas_call x0 -> x2, Pallas kernels: none -> 131 us  [the longest x1 115 us: layer(): pl.pallas_call(layer_kernel, name='layer', out_shape=(jax.ShapeDtypeStruc...]
    psum x1 -> x0, waiting for transfers between devices: 78.4 us -> none  [reduce_parts(): lax.psum(partial_term.astype(jnp.bfloat16), 'erow').astype(jnp.float32)]
    dot_general x10 -> x0, matrix products: 48.3 us -> none  [the longest x1 14.2 us: on_device(): jnp.einsum('rd,dgf->rgf', x_rows, w_in, preferred_element_type=jnp.float32)]
    all_to_all x6 -> x0, waiting for transfers between devices: 45 us -> none  [the longest x1 16.1 us: send_rows(): lax.all_to_all(cot_out, ('erow', 'ecol'), split_axis=0, concat_axis=0, ti...]
    all_to_all x6 -> x0, starting transfers between devices: 38 us -> none  [the longest x1 11.5 us: send_rows(): lax.all_to_all(prob_out, ('erow', 'ecol'), split_axis=0, concat_axis=0, t...]
    unnamed x24 -> x0, local copies, waits for them, and re-layouts: 22 us -> none
    reshape x9 -> x0, local copies, waits for them, and re-layouts: 9.16 us -> none  [the longest x1 2.53 us: return_values(): row_values.reshape(n_row * experts, capacity, weight_slice)]
    another operation x2 -> x0, other arithmetic: 4.18 us -> none
  transfers between devices with their start and end apart: 7 -> 0, of which waited for: 6 -> 0; matrix products, arithmetic and copies ran while one was open for 23% -> 0% of each run, Pallas kernels for 0% -> 0%
where the time goes in v1:
time: 132 us
  Pallas kernels  131 us (99%)
    pallas_call x1, Pallas kernels, layer(): pl.pallas_call(layer_kernel, name='layer', out_shape=(jax.ShapeDtypeStruc...  115 us
    pallas_call x1, Pallas kernels, weight_grads(): pl.pallas_call(grads_kernel, name='weight_grads', grid=(NR,), out_shape=(...  16.5 us

profile of v1, /device:TPU:1, one launch (start us, length us, event | category | flops | bytes accessed | tf_op | source)
XLA Modules:
  0.0 132.0 jit_solution(10427897920959383528)
XLA Ops:
  0.6 114.6 %layer.1 = (bf16[8,7168]{1,0:T(8,128)(2,1)}, bf16[8,7168]{1,0:T(8,128)(2,1)}, f32[4,8]{1,0:T(4,128)}, bf16[16,32,1792]{2,1,0:T(8,128)(2,1)}, bf16[8,512,768]{2,1,0:T(8,128)(2,1)}) custom-call(bf16[8,7168]{1,0:T(8,128)(2,1)} %tok.1, bf16[8,7168]{1,0:T(8,128)(2,1)} %cot.1, s32[4,8]{1,0:T(4,128)} %bitcast.5, bf16[4,8]{1,0:T(4,128)(2,1)} %bitcast.6, ...), custom_call_target="tpu_custom_call" | custom-call | tf_op jit(solution)/shard_map/layer/pallas_call | solution.py:457
  115.3 16.5 %weight_grads.1 = (bf16[1,2048,896]{2,1,0:T(8,128)(2,1)}, bf16[1,896,2,2048]{3,2,1,0:T(2,128)(2,1)}, bf16[8,7168]{1,0:T(8,128)(2,1)}, bf16[8,7168]{1,0:T(8,128)(2,1)}, f32[4,8]{1,0:T(4,128)}) custom-call(bf16[512,1792]{1,0:T(8,128)(2,1)} %bitcast.4, bf16[8,512,768]{2,1,0:T(8,128)(2,1)} %get-tuple-element.16.act_ref, ...), custom_call_target="tpu_custom_call" | custom-call | tf_op jit(solution)/shard_map/weight_grads/pallas_call | solution.py:527

commit v2 on v1

--- a/solution.py
+++ b/solution.py
@@ -20,10 +20,10 @@
 )
 BPQ = len(OFFSETS) // NQ
 SCHEDULE = (
-    "D0", "S0", "D1", "W0", "D2", "D3", "C0", "S1", "R0", "B0",
-    "S2", "C1", "A0", "R1", "B1", "S3", "F0", "C2", "A1", "R2",
-    "G0", "B2", "O0", "F1", "C3", "A2", "R3", "B3", "G1", "O1",
-    "F2", "A3", "G2", "O2", "F3", "K0", "G3", "O3", "K1", "K2",
+    "D0", "S0", "D2", "D1", "S1", "W0", "C0", "B0", "R0", "S2",
+    "C1", "D3", "S3", "A0", "R1", "F0", "C2", "B1", "A1", "G0",
+    "O0", "R2", "B2", "F1", "C3", "A2", "R3", "B3", "G1", "O1",
+    "F2", "A3", "K0", "G2", "O2", "F3", "G3", "O3", "K1", "K2",
     "K3",
 )
 

time: 132 us -> 132 us (level)
  no operation moved by 1% of the time
where the time goes in v2:
time: 132 us
  Pallas kernels  131 us (99%)
    pallas_call x1, Pallas kernels, layer(): pl.pallas_call(layer_kernel, name='layer', out_shape=(jax.ShapeDtypeStruc...  115 us
    pallas_call x1, Pallas kernels, weight_grads(): pl.pallas_call(grads_kernel, name='weight_grads', grid=(NR,), out_shape=(...  16.5 us

profile of v2, /device:TPU:1, one launch (start us, length us, event | category | flops | bytes accessed | tf_op | source)
XLA Modules:
  0.0 132.0 jit_solution(17069283896898323344)
XLA Ops:
  0.6 114.7 %layer.1 = (bf16[8,7168]{1,0:T(8,128)(2,1)}, bf16[8,7168]{1,0:T(8,128)(2,1)}, f32[4,8]{1,0:T(4,128)}, bf16[16,32,1792]{2,1,0:T(8,128)(2,1)}, bf16[8,512,768]{2,1,0:T(8,128)(2,1)}) custom-call(bf16[8,7168]{1,0:T(8,128)(2,1)} %tok.1, bf16[8,7168]{1,0:T(8,128)(2,1)} %cot.1, s32[4,8]{1,0:T(4,128)} %bitcast.5, bf16[4,8]{1,0:T(4,128)(2,1)} %bitcast.6, ...), custom_call_target="tpu_custom_call" | custom-call | tf_op jit(solution)/shard_map/layer/pallas_call | solution.py:457
  115.3 16.5 %weight_grads.1 = (bf16[1,2048,896]{2,1,0:T(8,128)(2,1)}, bf16[1,896,2,2048]{3,2,1,0:T(2,128)(2,1)}, bf16[8,7168]{1,0:T(8,128)(2,1)}, bf16[8,7168]{1,0:T(8,128)(2,1)}, f32[4,8]{1,0:T(4,128)}) custom-call(bf16[512,1792]{1,0:T(8,128)(2,1)} %bitcast.4, bf16[8,512,768]{2,1,0:T(8,128)(2,1)} %get-tuple-element.16.act_ref, ...), custom_call_target="tpu_custom_call" | custom-call | tf_op jit(solution)/shard_map/weight_grads/pallas_call | solution.py:527
